TPU v7x, 256 devices: a whole 4x4x8 slice. The times are simulated.
256 devices in a mesh: ctxa: 32 (over x, z), ctxb: 8 (over y, core).
Axes of the slice: x: 4, y: 4, z: 8, core: 2. Of those that a mesh axis runs over, the one named last changes fastest.
Arguments:
- tokens: bfloat16 [32768, 1024], P(('ctxa', 'ctxb')), may hold values from -80 to 80
- w_query: bfloat16 [1024, 512], replicated, may hold values from -0.1875 to 0.1875
- w_key: bfloat16 [1024, 512], replicated, may hold values from -0.1875 to 0.1875
- w_value: bfloat16 [1024, 512], replicated, may hold values from -0.1875 to 0.1875
- w_slot: bfloat16 [8, 64, 128], replicated, may hold values from -3 to 3
- w_out: bfloat16 [512, 1024], replicated, may hold values from -1 to 1
Outputs:
- mixed: bfloat16 [32768, 1024], P(('ctxa', 'ctxb'))
All inputs are finite; a program needn't handle non-finite values.
Results may differ from a plain program's by a relative error of at most 0.012.
The roundings to bfloat16 on the way count: a program that leaves them out, or rounds other values in their place, can miss the bound.
Values may be sent and summed in bfloat16 or wider, within the bound.
A program may use at most 192 MiB of HBM per device.

v0:
```python
import jax
import jax.numpy as jnp
from jax import lax
from jax.sharding import PartitionSpec as P

HEADS = 8
HEAD_DIM = 64
SLOTS = 128
WINDOW = 128


def padded_2(block, sides, width):
    for axis, dim in sides:
        count = lax.axis_size(axis)
        forward = [(i, i + 1) for i in range(count - 1)]
        backward = [(target, source) for source, target in forward]
        low = lax.ppermute(
            lax.slice_in_dim(block, block.shape[dim] - width, None, axis=dim), axis, forward
        )
        high = lax.ppermute(lax.slice_in_dim(block, 0, width, axis=dim), axis, backward)
        block = jnp.concatenate([low, block, high], axis=dim)
    return block


def layer_norm(values):
    center = values - jnp.mean(values, axis=-1, keepdims=True)
    spread = jnp.mean(center * center, axis=-1, keepdims=True)
    return center * lax.rsqrt(spread + 1e-05)


def finish_slots(total, sums):
    slot_keys = layer_norm(sums[..., :HEAD_DIM]).astype(jnp.bfloat16)
    slot_values = (sums[..., HEAD_DIM:] / total[..., None]).astype(jnp.bfloat16)
    return (slot_keys, slot_values)


def per_device(tokens, w_query, w_key, w_value, w_slot, w_out):
    rows = tokens.shape[0]
    width = HEADS * HEAD_DIM
    query = jnp.dot(tokens, w_query, preferred_element_type=jnp.float32).astype(jnp.bfloat16)
    key = jnp.dot(tokens, w_key, preferred_element_type=jnp.float32).astype(jnp.bfloat16)
    value = jnp.dot(tokens, w_value, preferred_element_type=jnp.float32).astype(jnp.bfloat16)
    key_heads = key.reshape(rows, HEADS, HEAD_DIM)
    logits = jnp.einsum("thd,hds->hts", key_heads, w_slot, preferred_element_type=jnp.float32)
    paired = jnp.concatenate([key_heads, value.reshape(rows, HEADS, HEAD_DIM)], axis=2).astype(
        jnp.float32
    )
    local_top = jnp.max(logits, axis=1)
    top = lax.pmax(local_top, ("ctxa", "ctxb"))
    weight = jnp.exp(logits - top[:, None, :])
    total = jnp.sum(weight, axis=1)
    sums = jnp.einsum("hts,thd->hsd", weight, paired, precision=lax.Precision.HIGHEST)
    total, sums = lax.psum((total, sums), ("ctxa", "ctxb"))
    slot_keys, slot_values = finish_slots(total, sums)
    near_keys = layer_norm(key_heads.astype(jnp.float32)).astype(jnp.bfloat16).reshape(rows, width)
    stacked = jnp.concatenate([near_keys, value], axis=1)
    padded = padded_2(stacked, ((("ctxa", "ctxb"), 0),), WINDOW)
    seq_len = rows * lax.axis_size(("ctxa", "ctxb"))
    offset = lax.axis_index(("ctxa", "ctxb")) * rows
    block = min(512, rows)
    span = block + 2 * WINDOW
    scale = 1.0 / HEAD_DIM**0.5
    groups = 2
    group_heads = HEADS // groups
    group_width = group_heads * HEAD_DIM
    grouped_keys = slot_keys.reshape(groups, group_heads, SLOTS, HEAD_DIM)
    grouped_values = slot_values.reshape(groups, group_heads, SLOTS, HEAD_DIM)
    blocks = rows // block

    def attend(item):
        index = item // groups
        group = item % groups
        start = index * block
        column = group * group_width
        query_block = lax.dynamic_slice_in_dim(query, column, group_width, 1).reshape(
            block, group_heads, HEAD_DIM
        )
        keys_block = lax.dynamic_slice_in_dim(padded, column, group_width, 1).reshape(
            span, group_heads, HEAD_DIM
        )
        values_block = lax.dynamic_slice_in_dim(padded, width + column, group_width, 1).reshape(
            span, group_heads, HEAD_DIM
        )
        group_slot_keys = lax.dynamic_index_in_dim(grouped_keys, group, 0, keepdims=False)
        group_slot_values = lax.dynamic_index_in_dim(grouped_values, group, 0, keepdims=False)
        query_pos = offset + start + jnp.arange(block, dtype=jnp.int32)
        key_pos = offset + start - WINDOW + jnp.arange(span, dtype=jnp.int32)
        valid = (
            (jnp.abs(key_pos[None, :] - query_pos[:, None]) <= WINDOW)
            & (key_pos[None, :] >= 0)
            & (key_pos[None, :] < seq_len)
        )
        near = (
            jnp.einsum("bhd,khd->hbk", query_block, keys_block, preferred_element_type=jnp.float32)
            * scale
        )
        near = jnp.where(valid[None], near, -1e30)
        far = (
            jnp.einsum(
                "bhd,hsd->hbs", query_block, group_slot_keys, preferred_element_type=jnp.float32
            )
            * scale
        )
        top_score = jnp.maximum(jnp.max(near, axis=-1), jnp.max(far, axis=-1))
        near_exp = jnp.exp(near - top_score[..., None])
        far_exp = jnp.exp(far - top_score[..., None])
        denom = jnp.sum(near_exp, axis=-1) + jnp.sum(far_exp, axis=-1)
        near_probs = (near_exp / denom[..., None]).astype(jnp.bfloat16)
        far_probs = (far_exp / denom[..., None]).astype(jnp.bfloat16)
        result = jnp.einsum(
            "hbk,khd->bhd", near_probs, values_block, preferred_element_type=jnp.float32
        )
        result = result + jnp.einsum(
            "hbs,hsd->bhd", far_probs, group_slot_values, preferred_element_type=jnp.float32
        )
        return result.reshape(block, group_width).astype(jnp.bfloat16)

    pieces = lax.map(attend, jnp.arange(blocks * groups, dtype=jnp.int32))
    attended = (
        pieces.reshape(blocks, groups, block, group_width)
        .transpose(0, 2, 1, 3)
        .reshape(rows, width)
    )
    return jnp.dot(attended, w_out, preferred_element_type=jnp.float32).astype(jnp.bfloat16)


def solution(mesh):
    in_specs = (P(("ctxa", "ctxb"), None), P(), P(), P(), P(), P())
    out_specs = P(("ctxa", "ctxb"), None)
    return jax.shard_map(
        per_device, mesh=mesh, in_specs=in_specs, out_specs=out_specs, check_vma=False
    )
```

profile of v0, /device:TPU:1, one launch (start us, length us, event | category | flops | bytes accessed | tf_op | source)
XLA Modules:
  0.0 377.4 jit_solution(4458475252980913308)
XLA Ops:
  6.5 1.8 convolution_convert_fusion.3
  8.5 0.3 convolution_convert_fusion.2
  9.3 0.7 pad_maximum_fusion.1
  10.0 4.6 %collective-permute-start = (bf16[128,1024]{1,0:T(8,128)(2,1)}, bf16[128,1024]{1,0:T(8,128)(2,1)}, u32[]{:S(2)}, u32[]{:S(2)}) collective-permute-start(bf16[128,1024]{1,0:T(8,128)(2,1)} %pad_maximum_fusion.1), channel_id=1, source_target_pairs={{0,1},{1,2},{2,3},{3,4},{4,5},{5,6},{6,7},{7,8},{8,9},{9,10},{10,1... | collective-permute-start | bytes 786440 | tf_op jit(solution)/shard_map/ppermute | solution.py:17
  14.6 2.5 collective-permute-start.1
  17.3 0.9 copy.21
  18.1 0.3 fusion.27
  18.4 79.8 %pmax.7 = f32[8,128]{1,0:T(8,128)S(1)} all-reduce(f32[8,128]{1,0:T(8,128)S(1)} %get-tuple-element.154), channel_id=1, replica_groups=mesh['ctxa'=32,'ctxb'=8] {'ctxa','ctxb'}, use_global_device_ids=true, to_apply=%region_3.0 | all-reduce | flops 1024 | bytes 8192 | tf_op jit(solution)/shard_map/pmax | solution.py:49
  98.2 0.2 copy.22
  98.4 2.5 fusion.17
  101.0 73.9 %psum.15 = f32[8,128]{1,0:T(8,128)S(1)} all-reduce(f32[8,128]{1,0:T(8,128)S(1)} %fusion.16), channel_id=1, replica_groups=mesh['ctxa'=32,'ctxb'=8] {'ctxa','ctxb'}, use_global_device_ids=true, to_apply=%region_8.0 | all-reduce | flops 1024 | bytes 8192 | tf_op jit(solution)/shard_map/psum | solution.py:53
  174.9 0.3 convolution_convert_fusion.1
  175.3 176.5 %all-reduce.2.cloned.1.call-done = f32[8,128,128]{2,1,0:T(8,128)} async-done(((f32[8,128,128]{2,1,0:T(8,128)}), f32[8,128,128]{2,1,0:T(8,128)}) %all-reduce.2.cloned.1.call-update) | async-done | bytes 524304 | tf_op jit(solution)/shard_map/psum | solution.py:53
  351.8 1.3 slice_reduce_fusion
  353.1 1.4 multiply_reduce_fusion
  354.5 0.6 fusion.15
  355.4 1.1 pad_maximum_fusion
  356.6 0.4 copy.24
  356.9 11.7 %while.12 = (s32[]{:T(128)}, bf16[2,128,256]{1,2,0:T(8,128)(2,1)}, s32[2]{0:T(128)S(1)}, bf16[384,1024]{0,1:T(8,128)(2,1)S(1)}, s32[]{:T(128)}, /*index=5*/bf16[...) while((s32[]{:T(128)}, bf16[2,128,256]{1,2,0:T(8,128)(2,1)}, ...), condition=%wide.region_14.15_spmd, body=%wide.region_9.14_spmd.sunk | while | flops 69452448 | bytes 5446203 | solution.py:118
  356.9 0.6 dynamic_slice.60
  360.5 0.4 fusion.63
  360.9 0.3 fusion.60
  361.3 0.3 fusion.64
  361.8 0.4 fusion.67
  362.2 0.6 constant_dynamic-update-slice_fusion.2
  362.8 0.6 dynamic_slice.60
  366.4 0.4 fusion.63
  366.8 0.3 fusion.60
  367.1 0.3 fusion.64
  367.6 0.4 fusion.67
  368.0 0.6 constant_dynamic-update-slice_fusion.2
  368.6 1.9 convolution_convert_fusion
  (56 shorter events, 2.2 us)
Async XLA Ops:
  6.5 362.1 %copy-start = (bf16[512,1024]{1,0:T(8,128)(2,1)S(1)}, bf16[512,1024]{1,0:T(8,128)(2,1)}, u32[]{:S(2)}) copy-start(bf16[512,1024]{1,0:T(8,128)(2,1)} %param.13) | copy-start | bytes 3145732
  6.5 1.9 copy-start.2
  6.5 1.9 copy-start.3
  6.5 345.2 %all-reduce.2.cloned.1.call-start = ((), (), s32[]{:S(2)}) async-start(), calls=%async_computation | async-start | bytes 1048576 | tf_op jit(solution)/shard_map/psum | solution.py:53
  9.2 8.9 %copy-start.5 = (bf16[8,64,128]{2,1,0:T(8,128)(2,1)S(1)}, bf16[8,64,128]{2,1,0:T(8,128)(2,1)}, u32[]{:S(2)}) copy-start(bf16[8,64,128]{2,1,0:T(8,128)(2,1)} %param.12) | copy-start | bytes 393220
  10.0 345.4 %collective-permute-start = (bf16[128,1024]{1,0:T(8,128)(2,1)}, bf16[128,1024]{1,0:T(8,128)(2,1)}, u32[]{:S(2)}, u32[]{:S(2)}) collective-permute-start(bf16[128,1024]{1,0:T(8,128)(2,1)} %pad_maximum_fusion.1), channel_id=1, source_target_pairs={{0,1},{1,2},{2,3},{3,4},{4,5},{5,6},{6,7},{7,8},{8,9},{9,10},{10,1... | collective-permute-start | bytes 786440 | tf_op jit(solution)/shard_map/ppermute | solution.py:17
  14.6 340.8 %collective-permute-start.1 = (bf16[128,1024]{1,0:T(8,128)(2,1)}, bf16[128,1024]{1,0:T(8,128)(2,1)}, u32[]{:S(2)}, u32[]{:S(2)}) collective-permute-start(bf16[128,1024]{1,0:T(8,128)(2,1)} %pad_maximum_fusion.1), channel_id=1, source_target_pairs={{1,0},{2,1},{3,2},{4,3},{5,4},{6,5},{7,6},{8,7},{9,8},{10,9},{11,1... | collective-permute-start | bytes 786440 | tf_op jit(solution)/shard_map/ppermute | solution.py:20
  98.4 76.6 %copy-start.4 = (bf16[1024,512]{1,0:T(8,128)(2,1)S(1)}, bf16[1024,512]{1,0:T(8,128)(2,1)}, u32[]{:S(2)}) copy-start(bf16[1024,512]{1,0:T(8,128)(2,1)} %param.9) | copy-start | bytes 3145732
  351.7 2.8 copy-start.1
Sparse Core Ops, SparseCore 0:
  101.0 250.6 all-reduce.1
where the time goes:
time: 379 us; the launch traced here: 377 us
  waiting for transfers between devices  177 us (47%)
  blocking collectives  154 us (41%)
  between operations  13.7 us (4%)
  matrix products  9.55 us (3%)
  starting transfers between devices  7.1 us (2%)
  other arithmetic  6.44 us (2%)
  loops' own time  5.47 us (1%)
  local copies, waits for them, and re-layouts  4.99 us (1%)
    psum x1, waiting for transfers between devices, per_device(): total, sums = lax.psum((total, sums), ('ctxa', 'ctxb'))  176 us
    pmax x1, blocking collectives, per_device(): top = lax.pmax(local_top, ('ctxa', 'ctxb'))  79.8 us
    psum x1, blocking collectives, per_device(): total, sums = lax.psum((total, sums), ('ctxa', 'ctxb'))  73.9 us
  transfers between devices with their start and end apart: 3, of which 1 were waited for; matrix products, arithmetic and copies ran while one was open for 2% of the time, Pallas kernels for 0%

commit v1 on v0

v1 whole, which is shorter than its diff:
```python
import jax
import jax.numpy as jnp
from jax import lax
from jax.experimental import pallas as pl
from jax.experimental.pallas import tpu as pltpu
from jax.sharding import PartitionSpec as P

HEADS = 8
HEAD_DIM = 64
SLOTS = 128
WINDOW = 128
ROWS = 128
D = 1024
WIDTH = HEADS * HEAD_DIM

NX = 4
NZ = 8
NB = 8
PLANE = NX * NB
DEVICES = PLANE * NZ
UNIT = 32
MSG = 40
SLOT_ROWS = 48

BF16 = jnp.bfloat16
F32 = jnp.float32
MESH = pl.DeviceIdType.MESH
NT = (((1,), (1,)), ((), ()))
TN = (((0,), (0,)), ((), ()))


def dot(a, b):
    return jnp.dot(a, b, preferred_element_type=F32)


def stats_block(top, total):
    row = lax.broadcasted_iota(jnp.int32, (8, SLOTS), 0)
    both = jnp.where(row < 3, top, total)
    high = both.astype(BF16).astype(F32)
    rest = both - high
    mid = rest.astype(BF16).astype(F32)
    low = rest - mid
    part = jnp.where(row < 3, row, row - 3)
    return jnp.where(part == 0, high, jnp.where(part == 1, mid, jnp.where(part == 2, low, 0.0)))


def merge(load_stats, load_data, count):
    stats = [load_stats(k).astype(F32) for k in range(count)]
    tops = [s[0:1] + s[1:2] + s[2:3] for s in stats]
    totals = [s[3:4] + s[4:5] + s[5:6] for s in stats]
    top = tops[0]
    for other in tops[1:]:
        top = jnp.maximum(top, other)
    total = jnp.zeros_like(top)
    sums = jnp.zeros((UNIT, SLOTS), F32)
    for k in range(count):
        scale = jnp.exp(tops[k] - top)
        total = total + scale * totals[k]
        sums = sums + scale * load_data(k).astype(F32)
    return top, total, sums


def layer(
    tok_hbm,
    wq_hbm,
    wk_hbm,
    wv_hbm,
    ws_hbm,
    wo_hbm,
    out_ref,
    tok,
    wq,
    wk,
    wv,
    ws,
    wo,
    in_sem,
    block_diag,
    key_ref,
    key_t,
    query_t,
    units,
    rs_in,
    z_out,
    z_in,
    slots,
    near,
    acc,
    near_top,
    near_sum,
    rs_send,
    rs_recv,
    z_send,
    z_recv,
    ag_send,
    ag_recv,
    halo_send,
    halo_recv,
):
    a = lax.axis_index("ctxa")
    b = lax.axis_index("ctxb")
    x = lax.div(a, NZ)
    z = lax.rem(a, NZ)
    me = x * NB + b
    line = a * NB + b

    copies = [
        pltpu.make_async_copy(src, dst, in_sem.at[i])
        for i, (src, dst) in enumerate(
            ((tok_hbm, tok), (wk_hbm, wk), (wv_hbm, wv), (ws_hbm, ws), (wq_hbm, wq), (wo_hbm, wo))
        )
    ]
    for copy in copies:
        copy.start()

    def plane_id(dx, db):
        tx = lax.rem(x + dx, NX)
        tb = lax.rem(b + db, NB)
        return tx, tb, (tx * NZ + z, tb)

    def line_id(step):
        other = lax.rem(line + step, DEVICES)
        return (lax.div(other, NB), lax.rem(other, NB))

    barrier = pltpu.get_barrier_semaphore()

    def greet_plane(k, carry):
        _, _, device = plane_id(lax.div(k, NB), lax.rem(k, NB))
        pl.semaphore_signal(barrier, inc=1, device_id=device, device_id_type=MESH)
        return carry

    def greet_z(k, carry):
        pl.semaphore_signal(
            barrier, inc=1, device_id=(x * NZ + lax.rem(z + k, NZ), b), device_id_type=MESH
        )
        return carry

    lax.fori_loop(1, PLANE, greet_plane, 0)
    lax.fori_loop(1, NZ, greet_z, 0)
    for step in (1, DEVICES - 1):
        pl.semaphore_signal(barrier, inc=1, device_id=line_id(step), device_id_type=MESH)

    def rs_copy(dx, db):
        tx, tb, device = plane_id(dx, db)
        slot = dx * NB + db
        return pltpu.make_async_remote_copy(
            src_ref=units.at[tx * NB + tb, pl.ds(0, MSG)],
            dst_ref=rs_in.at[slot, pl.ds(0, MSG)],
            send_sem=rs_send.at[slot],
            recv_sem=rs_recv.at[slot],
            device_id=device,
            device_id_type=MESH,
        )

    def z_copy(dz):
        return pltpu.make_async_remote_copy(
            src_ref=z_out.at[pl.ds(0, MSG)],
            dst_ref=z_in.at[dz, pl.ds(0, MSG)],
            send_sem=z_send.at[dz],
            recv_sem=z_recv.at[dz],
            device_id=(x * NZ + lax.rem(z + dz, NZ), b),
            device_id_type=MESH,
        )

    def ag_copy(dx, db):
        _, _, device = plane_id(dx, db)
        slot = dx * NB + db
        return pltpu.make_async_remote_copy(
            src_ref=slots.at[me],
            dst_ref=slots.at[me],
            send_sem=ag_send.at[slot],
            recv_sem=ag_recv.at[slot],
            device_id=device,
            device_id_type=MESH,
        )

    def halo_copy(side):
        return pltpu.make_async_remote_copy(
            src_ref=near.at[1],
            dst_ref=near.at[2 * side],
            send_sem=halo_send.at[side],
            recv_sem=halo_recv.at[side],
            device_id=line_id(1 if side == 0 else DEVICES - 1),
            device_id_type=MESH,
        )

    copies[0].wait()
    copies[1].wait()
    key = dot(tok[...], wk[...]).astype(BF16)
    key_ref[...] = key
    key_t[...] = key.T
    copies[2].wait()
    value_t = dot(tok[...], wv[...]).astype(BF16).T
    near[1, WIDTH:, :] = value_t
    copies[3].wait()
    zero = jnp.zeros((HEAD_DIM, SLOTS), BF16)
    for pair in range(HEADS // 2):
        block_diag[pair, 0:HEAD_DIM, 0:SLOTS] = ws[2 * pair]
        block_diag[pair, 0:HEAD_DIM, SLOTS:] = zero
        block_diag[pair, HEAD_DIM:, 0:SLOTS] = zero
        block_diag[pair, HEAD_DIM:, SLOTS:] = ws[2 * pair + 1]

    db_order = (4, 3, 5, 2, 6, 1, 7, 0)
    for step, dx in enumerate((2, 1, 3, 0)):
        pair = lax.rem(x + dx, NX)
        columns = pl.ds(pl.multiple_of(pair * 2 * HEAD_DIM, 2 * HEAD_DIM), 2 * HEAD_DIM)
        logits = dot(key_ref[:, columns], block_diag[pair])
        top = jnp.max(logits, axis=0, keepdims=True)
        weight = jnp.exp(logits - top)
        total = jnp.sum(weight, axis=0, keepdims=True)
        weight_high = weight.astype(BF16)
        weight_low = (weight - weight_high.astype(F32)).astype(BF16)
        for head in range(2):
            cols = slice(head * SLOTS, (head + 1) * SLOTS)
            high, low = weight_high[:, cols], weight_low[:, cols]
            first = pl.multiple_of(pair * 2 * HEAD_DIM + head * HEAD_DIM, HEAD_DIM)
            keys_h = key_t[pl.ds(first, HEAD_DIM), :]
            values_h = near[1, pl.ds(WIDTH + first, HEAD_DIM), :]
            key_sum = dot(keys_h, high) + dot(keys_h, low)
            key_sum = key_sum - jnp.mean(key_sum, axis=0, keepdims=True)
            value_sum = dot(values_h, high) + dot(values_h, low)
            stats = stats_block(top[:, cols], total[:, cols]).astype(BF16)
            for quarter, data in enumerate(
                (key_sum[:UNIT], key_sum[UNIT:], value_sum[:UNIT], value_sum[UNIT:])
            ):
                unit = pair * NB + head * 4 + quarter
                units[unit, 0:UNIT, :] = data.astype(BF16)
                units[unit, UNIT:MSG, :] = stats
        if step == 0:
            pl.semaphore_wait(barrier, PLANE + NZ)
        for db in db_order:
            if dx or db:
                rs_copy(dx, db).start()

    for head in range(HEADS):
        rows = slice(head * HEAD_DIM, (head + 1) * HEAD_DIM)
        values = key_t[rows, :].astype(F32)
        center = values - jnp.mean(values, axis=0, keepdims=True)
        spread = jnp.mean(center * center, axis=0, keepdims=True)
        near[1, rows, :] = (center * lax.rsqrt(spread + 1e-05)).astype(BF16)
    copies[4].wait()
    query = dot(tok[...], wq[...]).astype(BF16).astype(F32) * (1.0 / HEAD_DIM**0.5)
    query_t[...] = query.astype(BF16).T

    for slot in range(1, PLANE):
        rs_copy(slot // NB, slot % NB).wait_recv()

    rs_in[0, 0:MSG] = units[me, 0:MSG]
    top, total, sums = merge(
        lambda k: rs_in[k, UNIT:MSG, :], lambda k: rs_in[k, 0:UNIT, :], PLANE
    )
    z_out[0:UNIT, :] = sums.astype(BF16)
    z_out[UNIT:MSG, :] = stats_block(top, total).astype(BF16)
    for dz in (4, 3, 5, 2, 6, 1, 7):
        z_copy(dz).start()
    for side in range(2):
        halo_copy(side).start()
    for dz in range(1, NZ):
        z_copy(dz).wait_recv()
    z_in[0, 0:MSG] = z_out[0:MSG]
    top, total, sums = merge(lambda k: z_in[k, UNIT:MSG, :], lambda k: z_in[k, 0:UNIT, :], NZ)
    is_value = lax.rem(me, 4) >= 2
    divisor = jnp.where(is_value, total, 1.0)
    slots[me] = (sums / divisor).astype(BF16)
    for dx in (2, 1, 3, 0):
        for db in db_order:
            if dx or db:
                ag_copy(dx, db).start()

    for side in range(2):
        halo_copy(side).wait_recv()
    source = lax.broadcasted_iota(jnp.int32, (ROWS, ROWS), 0)
    target = lax.broadcasted_iota(jnp.int32, (ROWS, ROWS), 1)
    before = (source >= target) & (line > 0)
    after = (source <= target) & (line < DEVICES - 1)
    for head in range(HEADS):
        rows = slice(head * HEAD_DIM, (head + 1) * HEAD_DIM)
        value_rows = slice(WIDTH + head * HEAD_DIM, WIDTH + (head + 1) * HEAD_DIM)
        query_h = query_t[rows, :]
        scores = [
            lax.dot_general(near[i, rows, :], query_h, TN, preferred_element_type=F32)
            for i in range(3)
        ]
        scores[0] = jnp.where(before, scores[0], -1e30)
        scores[2] = jnp.where(after, scores[2], -1e30)
        top_h = jnp.max(
            jnp.maximum(jnp.maximum(scores[0], scores[1]), scores[2]), axis=0, keepdims=True
        )
        exps = [jnp.exp(s - top_h) for s in scores]
        near_top[head : head + 1, :] = top_h
        near_sum[head : head + 1, :] = jnp.sum(exps[0] + exps[1] + exps[2], axis=0, keepdims=True)
        total_h = dot(near[0, value_rows, :], exps[0].astype(BF16))
        total_h = total_h + dot(near[1, value_rows, :], exps[1].astype(BF16))
        acc[rows, :] = total_h + dot(near[2, value_rows, :], exps[2].astype(BF16))

    for slot in range(1, PLANE):
        ag_copy(slot // NB, slot % NB).wait_recv()

    copies[5].wait()
    attended = []
    for head in range(HEADS):
        rows = slice(head * HEAD_DIM, (head + 1) * HEAD_DIM)
        center = slots[4 * head : 4 * head + 2].reshape(HEAD_DIM, SLOTS).astype(F32)
        values_h = slots[4 * head + 2 : 4 * head + 4].reshape(HEAD_DIM, SLOTS)
        spread = jnp.mean(center * center, axis=0, keepdims=True)
        keys_h = (center * lax.rsqrt(spread + 1e-05)).astype(BF16)
        scores = lax.dot_general(keys_h, query_t[rows, :], TN, preferred_element_type=F32)
        top_n = near_top[head : head + 1, :]
        top_h = jnp.maximum(top_n, jnp.max(scores, axis=0, keepdims=True))
        exps = jnp.exp(scores - top_h)
        scale = jnp.exp(top_n - top_h)
        denom = scale * near_sum[head : head + 1, :] + jnp.sum(exps, axis=0, keepdims=True)
        result = scale * acc[rows, :] + dot(values_h, exps.astype(BF16))
        attended.append((result / denom).astype(BF16))
    attended = jnp.concatenate(attended, axis=0)
    out_ref[...] = lax.dot_general(
        attended, wo[...], TN, preferred_element_type=F32
    ).astype(BF16)

    for slot in range(1, PLANE):
        rs_copy(slot // NB, slot % NB).wait_send()
        ag_copy(slot // NB, slot % NB).wait_send()
    for dz in range(1, NZ):
        z_copy(dz).wait_send()
    for side in range(2):
        halo_copy(side).wait_send()


def per_device(tokens, w_query, w_key, w_value, w_slot, w_out):
    dma = pltpu.SemaphoreType.DMA
    return pl.pallas_call(
        layer,
        out_shape=jax.ShapeDtypeStruct((ROWS, D), BF16),
        in_specs=[pl.BlockSpec(memory_space=pl.ANY)] * 6,
        out_specs=pl.BlockSpec(memory_space=pltpu.VMEM),
        scratch_shapes=[
            pltpu.VMEM((ROWS, D), BF16),
            pltpu.VMEM((D, WIDTH), BF16),
            pltpu.VMEM((D, WIDTH), BF16),
            pltpu.VMEM((D, WIDTH), BF16),
            pltpu.VMEM((HEADS, HEAD_DIM, SLOTS), BF16),
            pltpu.VMEM((WIDTH, D), BF16),
            dma((6,)),
            pltpu.VMEM((HEADS // 2, 2 * HEAD_DIM, 2 * SLOTS), BF16),
            pltpu.VMEM((ROWS, WIDTH), BF16),
            pltpu.VMEM((WIDTH, ROWS), BF16),
            pltpu.VMEM((WIDTH, ROWS), BF16),
            pltpu.VMEM((PLANE, SLOT_ROWS, SLOTS), BF16),
            pltpu.VMEM((PLANE, SLOT_ROWS, SLOTS), BF16),
            pltpu.VMEM((SLOT_ROWS, SLOTS), BF16),
            pltpu.VMEM((NZ, SLOT_ROWS, SLOTS), BF16),
            pltpu.VMEM((PLANE, UNIT, SLOTS), BF16),
            pltpu.VMEM((3, 2 * WIDTH, ROWS), BF16),
            pltpu.VMEM((WIDTH, ROWS), F32),
            pltpu.VMEM((HEADS, ROWS), F32),
            pltpu.VMEM((HEADS, ROWS), F32),
            dma((PLANE,)),
            dma((PLANE,)),
            dma((NZ,)),
            dma((NZ,)),
            dma((PLANE,)),
            dma((PLANE,)),
            dma((2,)),
            dma((2,)),
        ],
        compiler_params=pltpu.CompilerParams(collective_id=0, has_side_effects=True),
        name="layer",
    )(tokens, w_query, w_key, w_value, w_slot, w_out)


def solution(mesh):
    in_specs = (P(("ctxa", "ctxb"), None), P(), P(), P(), P(), P())
    out_specs = P(("ctxa", "ctxb"), None)
    return jax.shard_map(
        per_device, mesh=mesh, in_specs=in_specs, out_specs=out_specs, check_vma=False
    )
```

time: 379 us -> 34.8 us (0.09)
  waiting for transfers between devices: 177 us -> 0 us
  blocking collectives: 154 us -> 0 us
  Pallas kernels: 0 us -> 33.1 us
  between operations: 13.7 us -> 0.01 us
  matrix products: 9.55 us -> 0 us
  starting transfers between devices: 7.1 us -> 0 us
  other arithmetic: 6.44 us -> 0 us
  loops' own time: 5.47 us -> 0 us
    psum x1 -> x0, waiting for transfers between devices: 176 us -> none  [per_device(): total, sums = lax.psum((total, sums), ('ctxa', 'ctxb'))]
    pmax x1 -> x0, blocking collectives: 79.8 us -> none  [per_device(): top = lax.pmax(local_top, ('ctxa', 'ctxb'))]
    psum x1 -> x0, blocking collectives: 73.9 us -> none  [per_device(): total, sums = lax.psum((total, sums), ('ctxa', 'ctxb'))]
    pallas_call x0 -> x1, Pallas kernels: none -> 33.1 us  [per_device(): pl.pallas_call(layer, out_shape=jax.ShapeDtypeStruct((ROWS, D), BF16), in...]
    dot_general x14 -> x0, matrix products: 9.55 us -> none  [the longest x1 2.52 us: per_device(): jnp.einsum('hts,thd->hsd', weight, paired, precision=lax.Precision.HIGHEST)]
    ppermute x2 -> x0, starting transfers between devices: 7.09 us -> none  [the longest x1 4.57 us: padded_2(): lax.ppermute(lax.slice_in_dim(block, block.shape[dim] - width, None, axis...]
    another operation x1 -> x0, loops' own time: 5.47 us -> none  [per_device(): pieces = lax.map(attend, jnp.arange(blocks * groups, dtype=jnp.int32))]
  transfers between devices with their start and end apart: 3 -> 0, of which waited for: 1 -> 0; matrix products, arithmetic and copies ran while one was open for 2% -> 0% of each run, Pallas kernels for 0% -> 0%
where the time goes in v1:
time: 34.8 us; the launch traced here: 34.7 us
  Pallas kernels  33.1 us (95%)
  local copies, waits for them, and re-layouts  1.67 us (5%)
    pallas_call x1, Pallas kernels, per_device(): pl.pallas_call(layer, out_shape=jax.ShapeDtypeStruct((ROWS, D), BF16), in...  33.1 us
    unnamed x1, local copies, waits for them, and re-layouts  1.67 us

profile of v1, /device:TPU:1, one launch (start us, length us, event | category | flops | bytes accessed | tf_op | source)
XLA Modules:
  0.0 34.7 jit_solution(15163102076766650628)
XLA Ops:
  0.0 33.1 %layer.1 = bf16[128,1024]{1,0:T(8,128)(2,1)} custom-call(bf16[128,1024]{1,0:T(8,128)(2,1)} %tok_hbm.1, bf16[1024,512]{1,0:T(8,128)(2,1)} %wq_hbm.1, bf16[1024,512]{1,0:T(8,128)(2,1)} %wk_hbm.1, bf16[1024,512]{1,0:T(8,128)(2,1)} %wv_hbm.1, bf16[8,64,128]{2,1,0:T(8,128)(2,1)} %ws_hbm.1, bf16[512,1024]{1,0:T(8,128)(2,1)} %wo_hbm.1), custom_call_target="tpu_custom_call" | custom-call | tf_op jit(solution)/shard_map/layer/pallas_call | solution.py:331
  33.1 1.7 %copy.8 = bf16[128,1024]{1,0:T(8,128)(2,1)} copy(bf16[128,1024]{1,0:T(8,128)(2,1)} %layer.1) | data formatting | bytes 524288

commit v2 on v1

v2 whole, which is shorter than its diff:
```python
import jax
import jax.numpy as jnp
from jax import lax
from jax.experimental import pallas as pl
from jax.experimental.pallas import tpu as pltpu
from jax.sharding import PartitionSpec as P

HEADS = 8
HEAD_DIM = 64
SLOTS = 128
WINDOW = 128
ROWS = 128
D = 1024
WIDTH = HEADS * HEAD_DIM

NX = 4
NZ = 8
NB = 8
PLANE = NX * NB
DEVICES = PLANE * NZ
UNIT = 32
MSG = 40
SLOT_ROWS = 48

BF16 = jnp.bfloat16
F32 = jnp.float32
MESH = pl.DeviceIdType.MESH
TN = (((0,), (0,)), ((), ()))


def dot(a, b):
    return jnp.dot(a, b, preferred_element_type=F32)


def stats_block(top, total):
    row = lax.broadcasted_iota(jnp.int32, (8, SLOTS), 0)
    both = jnp.where(row < 3, top, total)
    high = both.astype(BF16).astype(F32)
    rest = both - high
    mid = rest.astype(BF16).astype(F32)
    low = rest - mid
    part = jnp.where(row < 3, row, row - 3)
    return jnp.where(part == 0, high, jnp.where(part == 1, mid, jnp.where(part == 2, low, 0.0)))


def merge(parts, running=None):
    stats = [load_stats().astype(F32) for load_stats, _ in parts]
    tops = [s[0:1] + s[1:2] + s[2:3] for s in stats]
    totals = [s[3:4] + s[4:5] + s[5:6] for s in stats]
    top = tops[0]
    for other in tops[1:]:
        top = jnp.maximum(top, other)
    if running is None:
        total = jnp.zeros_like(top)
        sums = jnp.zeros((UNIT, SLOTS), F32)
    else:
        old_top, total, sums = running
        top = jnp.maximum(top, old_top)
        scale = jnp.exp(old_top - top)
        total, sums = scale * total, scale * sums
    for k, (_, load_data) in enumerate(parts):
        scale = jnp.exp(tops[k] - top)
        total = total + scale * totals[k]
        sums = sums + scale * load_data().astype(F32)
    return top, total, sums


def layer(
    tok_hbm,
    wq_hbm,
    wk_hbm,
    wv_hbm,
    ws_hbm,
    out_ref,
    tok,
    wq,
    wk,
    wv,
    ws,
    in_sem,
    block_diag,
    key_ref,
    key_t,
    query_t,
    units,
    rs_in,
    z_out,
    z_in,
    slots,
    near,
    relay,
    acc,
    near_top,
    near_sum,
    rs_send,
    rs_recv,
    z_send,
    z_recv,
    ag_send,
    ag_recv,
    halo_send,
    halo_recv,
    relay_send,
    relay_recv,
):
    a = lax.axis_index("ctxa")
    b = lax.axis_index("ctxb")
    x = a >> 3
    z = a & (NZ - 1)
    me = x * NB + b

    pairs = ((ws_hbm, ws), (tok_hbm, tok), (wk_hbm, wk), (wv_hbm, wv), (wq_hbm, wq))
    copies = [
        pltpu.make_async_copy(src, dst, in_sem.at[i]) for i, (src, dst) in enumerate(pairs)
    ]
    for copy in copies[:4]:
        copy.start()

    def device(dx=0, dz=0, db=0):
        return ((((x + dx) & (NX - 1)) << 3) | ((z + dz) & (NZ - 1)), (b + db) & (NB - 1))

    db_order = (4, 3, 5, 2, 6, 1, 7, 0)
    dz_order = (4, 3, 5, 2, 6, 1, 7)
    barrier = pltpu.get_barrier_semaphore()
    for dx in (2, 1, 3, 0):
        for db in db_order:
            if dx or db:
                pl.semaphore_signal(
                    barrier, inc=1, device_id=device(dx=dx, db=db), device_id_type=MESH
                )
    for dz in dz_order:
        pl.semaphore_signal(barrier, inc=1, device_id=device(dz=dz), device_id_type=MESH)

    def rs_copy(dx, db):
        unit = (((x + dx) & (NX - 1)) << 3) | ((b + db) & (NB - 1))
        return pltpu.make_async_remote_copy(
            src_ref=units.at[unit, pl.ds(0, MSG)],
            dst_ref=rs_in.at[dx * NB + db, pl.ds(0, MSG)],
            send_sem=rs_send.at[0],
            recv_sem=rs_recv.at[dx],
            device_id=device(dx=dx, db=db),
            device_id_type=MESH,
        )

    def z_copy(dz):
        return pltpu.make_async_remote_copy(
            src_ref=z_out.at[pl.ds(0, MSG)],
            dst_ref=z_in.at[dz, pl.ds(0, MSG)],
            send_sem=z_send.at[0],
            recv_sem=z_recv.at[0],
            device_id=device(dz=dz),
            device_id_type=MESH,
        )

    def ag_copy(dx, db):
        return pltpu.make_async_remote_copy(
            src_ref=slots.at[me],
            dst_ref=slots.at[me],
            send_sem=ag_send.at[0],
            recv_sem=ag_recv.at[dx],
            device_id=device(dx=dx, db=db),
            device_id_type=MESH,
        )

    def halo_copy(side, src, target):
        return pltpu.make_async_remote_copy(
            src_ref=src,
            dst_ref=near.at[2 * side],
            send_sem=halo_send.at[side],
            recv_sem=halo_recv.at[side],
            device_id=target,
            device_id_type=MESH,
        )

    def relay_copy(side):
        return pltpu.make_async_remote_copy(
            src_ref=near.at[1],
            dst_ref=relay,
            send_sem=relay_send.at[0],
            recv_sem=relay_recv.at[0],
            device_id=device(dz=1 if side == 0 else NZ - 1),
            device_id_type=MESH,
        )

    last, first = b == NB - 1, b == 0
    halo_next = halo_copy(0, near.at[1], device(db=1))
    halo_prev = halo_copy(1, near.at[1], device(db=NB - 1))
    cross_next = halo_copy(0, relay, device(dx=jnp.where(z == 0, 1, 0), db=1))
    cross_prev = halo_copy(1, relay, device(dx=jnp.where(z == NZ - 1, NX - 1, 0), db=NB - 1))

    def group_wait(ref, sem):
        pltpu.make_async_copy(ref, ref, sem).wait()

    copies[0].wait()
    zero = jnp.zeros((HEAD_DIM, SLOTS), BF16)
    for pair in range(HEADS // 2):
        block_diag[pair, 0:HEAD_DIM, 0:SLOTS] = ws[2 * pair]
        block_diag[pair, 0:HEAD_DIM, SLOTS:] = zero
        block_diag[pair, HEAD_DIM:, 0:SLOTS] = zero
        block_diag[pair, HEAD_DIM:, SLOTS:] = ws[2 * pair + 1]
    copies[1].wait()
    copies[2].wait()
    key = dot(tok[...], wk[...]).astype(BF16)
    copies[4].start()
    key_ref[...] = key
    key_t[...] = key.T
    copies[3].wait()
    near[1, WIDTH:, :] = dot(tok[...], wv[...]).astype(BF16).T

    for step, dx in enumerate((2, 1, 3, 0)):
        pair = (x + dx) & (NX - 1)
        columns = pl.ds(pl.multiple_of(pair * 2 * HEAD_DIM, 2 * HEAD_DIM), 2 * HEAD_DIM)
        logits = dot(key_ref[:, columns], block_diag[pair])
        top = jnp.max(logits, axis=0, keepdims=True)
        weight = jnp.exp(logits - top)
        total = jnp.sum(weight, axis=0, keepdims=True)
        weight_high = weight.astype(BF16)
        weight_low = (weight - weight_high.astype(F32)).astype(BF16)
        for head in range(2):
            cols = slice(head * SLOTS, (head + 1) * SLOTS)
            high, low = weight_high[:, cols], weight_low[:, cols]
            start = pl.multiple_of(pair * 2 * HEAD_DIM + head * HEAD_DIM, HEAD_DIM)
            keys_h = key_t[pl.ds(start, HEAD_DIM), :]
            values_h = near[1, pl.ds(WIDTH + start, HEAD_DIM), :]
            key_sum = dot(keys_h, high) + dot(keys_h, low)
            key_sum = key_sum - jnp.mean(key_sum, axis=0, keepdims=True)
            value_sum = dot(values_h, high) + dot(values_h, low)
            stats = stats_block(top[:, cols], total[:, cols]).astype(BF16)
            for quarter, data in enumerate(
                (key_sum[:UNIT], key_sum[UNIT:], value_sum[:UNIT], value_sum[UNIT:])
            ):
                unit = pair * NB + head * 4 + quarter
                units[unit, 0:UNIT, :] = data.astype(BF16)
                units[unit, UNIT:MSG, :] = stats
        if step == 0:
            pl.semaphore_wait(barrier, PLANE + NZ - 2)
        for db in db_order:
            if dx or db:
                rs_copy(dx, db).start()

    for head in range(HEADS):
        rows = slice(head * HEAD_DIM, (head + 1) * HEAD_DIM)
        values = key_t[rows, :].astype(F32)
        center = values - jnp.mean(values, axis=0, keepdims=True)
        spread = jnp.mean(center * center, axis=0, keepdims=True)
        near[1, rows, :] = (center * lax.rsqrt(spread + 1e-05)).astype(BF16)
    pl.when(last)(lambda: relay_copy(0).start())
    pl.when(first)(lambda: relay_copy(1).start())
    copies[4].wait()
    query = dot(tok[...], wq[...]).astype(BF16).astype(F32) * (1.0 / HEAD_DIM**0.5)
    query_t[...] = query.astype(BF16).T

    running = None
    for dx in (0, 1, 3, 2):
        low = 1 if dx == 0 else 0
        group_wait(rs_in.at[pl.ds(dx * NB + low, NB - low), pl.ds(0, MSG)], rs_recv.at[dx])
        parts = [
            (lambda k=k: rs_in[k, UNIT:MSG, :], lambda k=k: rs_in[k, 0:UNIT, :])
            for k in range(dx * NB + low, (dx + 1) * NB)
        ]
        if dx == 0:
            parts.append((lambda: units[me, UNIT:MSG, :], lambda: units[me, 0:UNIT, :]))
        running = merge(parts, running)
    top, total, sums = running
    z_out[0:UNIT, :] = sums.astype(BF16)
    z_out[UNIT:MSG, :] = stats_block(top, total).astype(BF16)
    for dz in dz_order:
        z_copy(dz).start()

    @pl.when(last)
    def _():
        relay_copy(0).wait_recv()
        cross_next.start()

    @pl.when(first)
    def _():
        relay_copy(1).wait_recv()
        cross_prev.start()

    pl.when(jnp.logical_not(last))(halo_next.start)
    pl.when(jnp.logical_not(first))(halo_prev.start)
    group_wait(z_in.at[pl.ds(1, NZ - 1), pl.ds(0, MSG)], z_recv.at[0])
    parts = [
        (lambda k=k: z_in[k, UNIT:MSG, :], lambda k=k: z_in[k, 0:UNIT, :]) for k in range(1, NZ)
    ]
    parts.append((lambda: z_out[UNIT:MSG, :], lambda: z_out[0:UNIT, :]))
    top, total, sums = merge(parts)
    divisor = jnp.where((b & 3) >= 2, total, 1.0)
    slots[me] = (sums / divisor).astype(BF16)
    for dx in (2, 1, 3, 0):
        for db in db_order:
            if dx or db:
                ag_copy(dx, db).start()

    halo_next.wait_recv()
    halo_prev.wait_recv()
    source = lax.broadcasted_iota(jnp.int32, (ROWS, ROWS), 0)
    target = lax.broadcasted_iota(jnp.int32, (ROWS, ROWS), 1)
    line = a * NB + b
    before = (source >= target) & (line > 0)
    after = (source <= target) & (line < DEVICES - 1)
    for head in range(HEADS):
        rows = slice(head * HEAD_DIM, (head + 1) * HEAD_DIM)
        value_rows = slice(WIDTH + head * HEAD_DIM, WIDTH + (head + 1) * HEAD_DIM)
        query_h = query_t[rows, :]
        scores = [
            lax.dot_general(near[i, rows, :], query_h, TN, preferred_element_type=F32)
            for i in range(3)
        ]
        scores[0] = jnp.where(before, scores[0], -1e30)
        scores[2] = jnp.where(after, scores[2], -1e30)
        top_h = jnp.max(
            jnp.maximum(jnp.maximum(scores[0], scores[1]), scores[2]), axis=0, keepdims=True
        )
        exps = [jnp.exp(s - top_h) for s in scores]
        near_top[head] = jnp.broadcast_to(top_h, (8, ROWS))
        near_sum[head] = jnp.broadcast_to(
            jnp.sum(exps[0] + exps[1] + exps[2], axis=0, keepdims=True), (8, ROWS)
        )
        total_h = dot(near[0, value_rows, :], exps[0].astype(BF16))
        total_h = total_h + dot(near[1, value_rows, :], exps[1].astype(BF16))
        acc[rows, :] = total_h + dot(near[2, value_rows, :], exps[2].astype(BF16))

    for dx in (0, 1, 3, 2):
        low = 1 if dx == 0 else 0
        group_wait(slots.at[pl.ds(0, NB - low)], ag_recv.at[dx])
        pair = (x + NX - dx) & (NX - 1)
        results = []
        for half in range(2):
            head = pair * 2 + half
            start = pl.multiple_of(head * HEAD_DIM, HEAD_DIM)
            center = slots[pl.ds(4 * head, 2)].reshape(HEAD_DIM, SLOTS).astype(F32)
            values_h = slots[pl.ds(4 * head + 2, 2)].reshape(HEAD_DIM, SLOTS)
            spread = jnp.mean(center * center, axis=0, keepdims=True)
            keys_h = (center * lax.rsqrt(spread + 1e-05)).astype(BF16)
            scores = lax.dot_general(
                keys_h, query_t[pl.ds(start, HEAD_DIM), :], TN, preferred_element_type=F32
            )
            top_n = near_top[head, 0:1, :]
            top_h = jnp.maximum(top_n, jnp.max(scores, axis=0, keepdims=True))
            exps = jnp.exp(scores - top_h)
            scale = jnp.exp(top_n - top_h)
            denom = scale * near_sum[head, 0:1, :] + jnp.sum(exps, axis=0, keepdims=True)
            result = scale * acc[pl.ds(start, HEAD_DIM), :] + dot(values_h, exps.astype(BF16))
            results.append((result / denom).astype(BF16))
        columns = pl.ds(pl.multiple_of(pair * 2 * HEAD_DIM, 2 * HEAD_DIM), 2 * HEAD_DIM)
        out_ref[:, columns] = jnp.concatenate(results, axis=0).T

    group_wait(rs_in.at[pl.ds(0, PLANE - 1), pl.ds(0, MSG)], rs_send.at[0])
    group_wait(z_in.at[pl.ds(0, NZ - 1), pl.ds(0, MSG)], z_send.at[0])
    group_wait(slots.at[pl.ds(0, PLANE - 1)], ag_send.at[0])
    halo_next.wait_send()
    halo_prev.wait_send()
    pl.when(last | first)(relay_copy(0).wait_send)


def per_device(tokens, w_query, w_key, w_value, w_slot, w_out):
    dma = pltpu.SemaphoreType.DMA
    attended = pl.pallas_call(
        layer,
        out_shape=jax.ShapeDtypeStruct((ROWS, WIDTH), BF16),
        in_specs=[pl.BlockSpec(memory_space=pltpu.HBM)] * 5,
        out_specs=pl.BlockSpec(memory_space=pltpu.VMEM),
        scratch_shapes=[
            pltpu.VMEM((ROWS, D), BF16),
            pltpu.VMEM((D, WIDTH), BF16),
            pltpu.VMEM((D, WIDTH), BF16),
            pltpu.VMEM((D, WIDTH), BF16),
            pltpu.VMEM((HEADS, HEAD_DIM, SLOTS), BF16),
            dma((5,)),
            pltpu.VMEM((HEADS // 2, 2 * HEAD_DIM, 2 * SLOTS), BF16),
            pltpu.VMEM((ROWS, WIDTH), BF16),
            pltpu.VMEM((WIDTH, ROWS), BF16),
            pltpu.VMEM((WIDTH, ROWS), BF16),
            pltpu.VMEM((PLANE, SLOT_ROWS, SLOTS), BF16),
            pltpu.VMEM((PLANE, SLOT_ROWS, SLOTS), BF16),
            pltpu.VMEM((SLOT_ROWS, SLOTS), BF16),
            pltpu.VMEM((NZ, SLOT_ROWS, SLOTS), BF16),
            pltpu.VMEM((PLANE, UNIT, SLOTS), BF16),
            pltpu.VMEM((3, 2 * WIDTH, ROWS), BF16),
            pltpu.VMEM((2 * WIDTH, ROWS), BF16),
            pltpu.VMEM((WIDTH, ROWS), F32),
            pltpu.VMEM((HEADS, 8, ROWS), F32),
            pltpu.VMEM((HEADS, 8, ROWS), F32),
            dma((1,)),
            dma((NX,)),
            dma((1,)),
            dma((1,)),
            dma((1,)),
            dma((NX,)),
            dma((2,)),
            dma((2,)),
            dma((1,)),
            dma((1,)),
        ],
        compiler_params=pltpu.CompilerParams(
            collective_id=0, has_side_effects=True, vmem_limit_bytes=24 * 1024 * 1024
        ),
        name="layer",
    )(*(pltpu.with_memory_space_constraint(v, pltpu.HBM) for v in (tokens, w_query, w_key, w_value, w_slot)))
    return jnp.dot(attended, w_out, preferred_element_type=F32).astype(BF16)


def solution(mesh):
    in_specs = (P(("ctxa", "ctxb"), None), P(), P(), P(), P(), P())
    out_specs = P(("ctxa", "ctxb"), None)
    return jax.shard_map(
        per_device, mesh=mesh, in_specs=in_specs, out_specs=out_specs, check_vma=False
    )
```

time: 34.8 us -> 30.6 us (0.88)
  Pallas kernels: 33.1 us -> 29.5 us
  local copies, waits for them, and re-layouts: 1.67 us -> 0.01 us
  matrix products: 0 us -> 1.01 us
    pallas_call x1, Pallas kernels: 33.1 us -> 29.5 us  [per_device(): pl.pallas_call(layer, out_shape=jax.ShapeDtypeStruct((ROWS, WIDTH), BF16)...]
    unnamed x1 -> x2, local copies, waits for them, and re-layouts: 1.67 us -> 0.01 us
    dot_general x0 -> x1, matrix products: none -> 1.01 us  [per_device(): return jnp.dot(attended, w_out, preferred_element_type=F32).astype(BF16)]
where the time goes in v2:
time: 30.6 us
  Pallas kernels  29.5 us (96%)
  matrix products  1.01 us (3%)
    pallas_call x1, Pallas kernels, per_device(): pl.pallas_call(layer, out_shape=jax.ShapeDtypeStruct((ROWS, WIDTH), BF16)...  29.5 us
    dot_general x1, matrix products, per_device(): return jnp.dot(attended, w_out, preferred_element_type=F32).astype(BF16)  1.01 us

profile of v2, /device:TPU:1, one launch (start us, length us, event | category | flops | bytes accessed | tf_op | source)
XLA Modules:
  0.0 30.6 jit_solution(13718913450474556414)
XLA Ops:
  0.0 0.0 copy-start
  0.0 29.5 %layer.1 = bf16[128,512]{1,0:T(8,128)(2,1)S(1)} custom-call(bf16[128,1024]{1,0:T(8,128)(2,1)} %tok_hbm.1, bf16[1024,512]{1,0:T(8,128)(2,1)} %wq_hbm.1, bf16[1024,512]{1,0:T(8,128)(2,1)} %wk_hbm.1, bf16[1024,512]{1,0:T(8,128)(2,1)} %wv_hbm.1, bf16[8,64,128]{2,1,0:T(8,128)(2,1)} %ws_hbm.1), custom_call_target="tpu_custom_call" | custom-call | tf_op jit(solution)/shard_map/layer/pallas_call | solution.py:359
  29.5 0.0 copy-done
  29.6 1.0 %convolution_convert_fusion = bf16[128,1024]{1,0:T(8,128)(2,1)} fusion(bf16[128,512]{1,0:T(8,128)(2,1)S(1)} %layer.1, bf16[512,1024]{1,0:T(8,128)(2,1)S(1)} %copy-done), kind=kOutput, calls=%fused_computation | convolution fusion | flops 134348800 | bytes 1441792 | tf_op jit(solution)/shard_map/dot_general | solution.py:401
Async XLA Ops:
  0.0 29.5 %copy-start = (bf16[512,1024]{1,0:T(8,128)(2,1)S(1)}, bf16[512,1024]{1,0:T(8,128)(2,1)}, u32[]{:S(2)}) copy-start(bf16[512,1024]{1,0:T(8,128)(2,1)} %param.11) | copy-start | bytes 3145732

commit v3 on v2

--- a/solution.py
+++ b/solution.py
@@ -201,30 +201,37 @@
     copies[1].wait()
     copies[2].wait()
     key = dot(tok[...], wk[...]).astype(BF16)
-    copies[4].start()
     key_ref[...] = key
     key_t[...] = key.T
     copies[3].wait()
     near[1, WIDTH:, :] = dot(tok[...], wv[...]).astype(BF16).T
-
-    for step, dx in enumerate((2, 1, 3, 0)):
+    copies[4].start()
+
+    dx_order = (2, 1, 3, 0)
+
+    def send(dx):
+        for db in db_order:
+            if dx or db:
+                rs_copy(dx, db).start()
+
+    def pair_sums(dx):
         pair = (x + dx) & (NX - 1)
         columns = pl.ds(pl.multiple_of(pair * 2 * HEAD_DIM, 2 * HEAD_DIM), 2 * HEAD_DIM)
         logits = dot(key_ref[:, columns], block_diag[pair])
         top = jnp.max(logits, axis=0, keepdims=True)
         weight = jnp.exp(logits - top)
         total = jnp.sum(weight, axis=0, keepdims=True)
-        weight_high = weight.astype(BF16)
-        weight_low = (weight - weight_high.astype(F32)).astype(BF16)
+        weight = weight.astype(BF16)
         for head in range(2):
             cols = slice(head * SLOTS, (head + 1) * SLOTS)
-            high, low = weight_high[:, cols], weight_low[:, cols]
             start = pl.multiple_of(pair * 2 * HEAD_DIM + head * HEAD_DIM, HEAD_DIM)
-            keys_h = key_t[pl.ds(start, HEAD_DIM), :]
-            values_h = near[1, pl.ds(WIDTH + start, HEAD_DIM), :]
-            key_sum = dot(keys_h, high) + dot(keys_h, low)
+            paired = jnp.concatenate(
+                [key_t[pl.ds(start, HEAD_DIM), :], near[1, pl.ds(WIDTH + start, HEAD_DIM), :]],
+                axis=0,
+            )
+            sums = dot(paired, weight[:, cols])
+            key_sum, value_sum = sums[:HEAD_DIM], sums[HEAD_DIM:]
             key_sum = key_sum - jnp.mean(key_sum, axis=0, keepdims=True)
-            value_sum = dot(values_h, high) + dot(values_h, low)
             stats = stats_block(top[:, cols], total[:, cols]).astype(BF16)
             for quarter, data in enumerate(
                 (key_sum[:UNIT], key_sum[UNIT:], value_sum[:UNIT], value_sum[UNIT:])
@@ -232,12 +239,16 @@
                 unit = pair * NB + head * 4 + quarter
                 units[unit, 0:UNIT, :] = data.astype(BF16)
                 units[unit, UNIT:MSG, :] = stats
-        if step == 0:
-            pl.semaphore_wait(barrier, PLANE + NZ - 2)
-        for db in db_order:
-            if dx or db:
-                rs_copy(dx, db).start()
-
+
+    pair_sums(2)
+    pl.semaphore_wait(barrier, PLANE + NZ - 2)
+    send(2)
+    pair_sums(1)
+    send(1)
+    pair_sums(3)
+    send(3)
+    pair_sums(0)
+    send(0)
     for head in range(HEADS):
         rows = slice(head * HEAD_DIM, (head + 1) * HEAD_DIM)
         values = key_t[rows, :].astype(F32)

time: 30.6 us -> 29.9 us (0.977)
  Pallas kernels: 29.5 us -> 28.7 us
    pallas_call x1, Pallas kernels: 29.5 us -> 28.7 us  [per_device(): pl.pallas_call(layer, out_shape=jax.ShapeDtypeStruct((ROWS, WIDTH), BF16)...]
where the time goes in v3:
time: 29.9 us; the launch traced here: 29.8 us
  Pallas kernels  28.7 us (96%)
  matrix products  1.02 us (3%)
    pallas_call x1, Pallas kernels, per_device(): pl.pallas_call(layer, out_shape=jax.ShapeDtypeStruct((ROWS, WIDTH), BF16)...  28.7 us
    dot_general x1, matrix products, per_device(): return jnp.dot(attended, w_out, preferred_element_type=F32).astype(BF16)  1.02 us

profile of v3, /device:TPU:1, one launch (start us, length us, event | category | flops | bytes accessed | tf_op | source)
XLA Modules:
  0.0 29.8 jit_solution(8315246244348183286)
XLA Ops:
  0.0 0.0 copy-start
  0.0 28.7 %layer.1 = bf16[128,512]{1,0:T(8,128)(2,1)S(1)} custom-call(bf16[128,1024]{1,0:T(8,128)(2,1)} %tok_hbm.1, bf16[1024,512]{1,0:T(8,128)(2,1)} %wq_hbm.1, bf16[1024,512]{1,0:T(8,128)(2,1)} %wk_hbm.1, bf16[1024,512]{1,0:T(8,128)(2,1)} %wv_hbm.1, bf16[8,64,128]{2,1,0:T(8,128)(2,1)} %ws_hbm.1), custom_call_target="tpu_custom_call" | custom-call | tf_op jit(solution)/shard_map/layer/pallas_call | solution.py:370
  28.8 0.0 copy-done
  28.8 1.0 %convolution_convert_fusion = bf16[128,1024]{1,0:T(8,128)(2,1)} fusion(bf16[128,512]{1,0:T(8,128)(2,1)S(1)} %layer.1, bf16[512,1024]{1,0:T(8,128)(2,1)S(1)} %copy-done), kind=kOutput, calls=%fused_computation | convolution fusion | flops 134348800 | bytes 1441792 | tf_op jit(solution)/shard_map/dot_general | solution.py:412
Async XLA Ops:
  0.0 28.8 %copy-start = (bf16[512,1024]{1,0:T(8,128)(2,1)S(1)}, bf16[512,1024]{1,0:T(8,128)(2,1)}, u32[]{:S(2)}) copy-start(bf16[512,1024]{1,0:T(8,128)(2,1)} %param.11) | copy-start | bytes 3145732

commit v4 on v2

--- a/solution.py
+++ b/solution.py
@@ -16,7 +16,9 @@
 NX = 4
 NZ = 8
 NB = 8
+NY = 4
 PLANE = NX * NB
+CHIPS = NX * NY
 DEVICES = PLANE * NZ
 UNIT = 32
 MSG = 40
@@ -78,9 +80,8 @@
     wv,
     ws,
     in_sem,
-    block_diag,
-    key_ref,
-    key_t,
+    kv_t,
+    other_t,
     query_t,
     units,
     rs_in,
@@ -92,6 +93,11 @@
     acc,
     near_top,
     near_sum,
+    column,
+    upward,
+    downward,
+    swap_send,
+    swap_recv,
     rs_send,
     rs_recv,
     z_send,
@@ -107,7 +113,9 @@
     b = lax.axis_index("ctxb")
     x = a >> 3
     z = a & (NZ - 1)
-    me = x * NB + b
+    y = b >> 1
+    c = b & 1
+    me = x * NB + c * 4 + y
 
     pairs = ((ws_hbm, ws), (tok_hbm, tok), (wk_hbm, wk), (wv_hbm, wv), (wq_hbm, wq))
     copies = [
@@ -122,23 +130,41 @@
     db_order = (4, 3, 5, 2, 6, 1, 7, 0)
     dz_order = (4, 3, 5, 2, 6, 1, 7)
     barrier = pltpu.get_barrier_semaphore()
-    for dx in (2, 1, 3, 0):
-        for db in db_order:
-            if dx or db:
-                pl.semaphore_signal(
-                    barrier, inc=1, device_id=device(dx=dx, db=db), device_id_type=MESH
-                )
-    for dz in dz_order:
-        pl.semaphore_signal(barrier, inc=1, device_id=device(dz=dz), device_id_type=MESH)
-
-    def rs_copy(dx, db):
-        unit = (((x + dx) & (NX - 1)) << 3) | ((b + db) & (NB - 1))
+    greeted = [device(dx=2), device(db=4), (a, b + 1 - 2 * c), device(dz=1), device(dz=NZ - 1)]
+    greeted += [device(dx=1), device(dx=3), device(db=2), device(db=6)]
+    for other in greeted:
+        pl.semaphore_signal(barrier, inc=1, device_id=other, device_id_type=MESH)
+
+    def pass_on(sem, to):
+        pl.semaphore_signal(sem, inc=1, device_id=device(dz=to), device_id_type=MESH)
+
+    def wait_greetings():
+        pl.semaphore_wait(barrier, len(greeted))
+        for dx in (2, 1, 3):
+            pl.semaphore_signal(
+                column.at[NX - dx], inc=1, device_id=device(dx=dx), device_id_type=MESH
+            )
+        pass_on(upward.at[0], 1)
+        pass_on(downward.at[0], NZ - 1)
+
+    def swap_copy(i):
+        return pltpu.make_async_remote_copy(
+            src_ref=kv_t.at[i, :, 1 - c],
+            dst_ref=other_t.at[i],
+            send_sem=swap_send.at[i],
+            recv_sem=swap_recv.at[i],
+            device_id=(a, b + 1 - 2 * c),
+            device_id_type=MESH,
+        )
+
+    def rs_copy(dx, dy):
+        unit = (((x + dx) & (NX - 1)) << 2) | ((y + dy) & (NY - 1))
         return pltpu.make_async_remote_copy(
             src_ref=units.at[unit, pl.ds(0, MSG)],
-            dst_ref=rs_in.at[dx * NB + db, pl.ds(0, MSG)],
+            dst_ref=rs_in.at[dx * NY + dy, pl.ds(0, MSG)],
             send_sem=rs_send.at[0],
             recv_sem=rs_recv.at[dx],
-            device_id=device(dx=dx, db=db),
+            device_id=device(dx=dx, db=2 * dy),
             device_id_type=MESH,
         )
 
@@ -191,75 +217,89 @@
     def group_wait(ref, sem):
         pltpu.make_async_copy(ref, ref, sem).wait()
 
-    copies[0].wait()
-    zero = jnp.zeros((HEAD_DIM, SLOTS), BF16)
-    for pair in range(HEADS // 2):
-        block_diag[pair, 0:HEAD_DIM, 0:SLOTS] = ws[2 * pair]
-        block_diag[pair, 0:HEAD_DIM, SLOTS:] = zero
-        block_diag[pair, HEAD_DIM:, 0:SLOTS] = zero
-        block_diag[pair, HEAD_DIM:, SLOTS:] = ws[2 * pair + 1]
+    def block_weights(keys_h, slot_map):
+        logits = lax.dot_general(keys_h, slot_map, TN, preferred_element_type=F32)
+        top = jnp.max(logits, axis=0, keepdims=True)
+        weight = jnp.exp(logits - top)
+        return top, jnp.sum(weight, axis=0, keepdims=True), weight.astype(BF16)
+
     copies[1].wait()
     copies[2].wait()
-    key = dot(tok[...], wk[...]).astype(BF16)
+    kv_t[0] = dot(tok[...], wk[...]).astype(BF16).T.reshape(NX, 2, HEAD_DIM, ROWS)
+    copies[3].wait()
+    value_t = dot(tok[...], wv[...]).astype(BF16).T
+    kv_t[1] = value_t.reshape(NX, 2, HEAD_DIM, ROWS)
+    wait_greetings()
+    swap_copy(0).start()
+    swap_copy(1).start()
     copies[4].start()
-    key_ref[...] = key
-    key_t[...] = key.T
-    copies[3].wait()
-    near[1, WIDTH:, :] = dot(tok[...], wv[...]).astype(BF16).T
-
-    for step, dx in enumerate((2, 1, 3, 0)):
-        pair = (x + dx) & (NX - 1)
-        columns = pl.ds(pl.multiple_of(pair * 2 * HEAD_DIM, 2 * HEAD_DIM), 2 * HEAD_DIM)
-        logits = dot(key_ref[:, columns], block_diag[pair])
-        top = jnp.max(logits, axis=0, keepdims=True)
-        weight = jnp.exp(logits - top)
-        total = jnp.sum(weight, axis=0, keepdims=True)
-        weight_high = weight.astype(BF16)
-        weight_low = (weight - weight_high.astype(F32)).astype(BF16)
-        for head in range(2):
-            cols = slice(head * SLOTS, (head + 1) * SLOTS)
-            high, low = weight_high[:, cols], weight_low[:, cols]
-            start = pl.multiple_of(pair * 2 * HEAD_DIM + head * HEAD_DIM, HEAD_DIM)
-            keys_h = key_t[pl.ds(start, HEAD_DIM), :]
-            values_h = near[1, pl.ds(WIDTH + start, HEAD_DIM), :]
-            key_sum = dot(keys_h, high) + dot(keys_h, low)
-            key_sum = key_sum - jnp.mean(key_sum, axis=0, keepdims=True)
-            value_sum = dot(values_h, high) + dot(values_h, low)
-            stats = stats_block(top[:, cols], total[:, cols]).astype(BF16)
-            for quarter, data in enumerate(
-                (key_sum[:UNIT], key_sum[UNIT:], value_sum[:UNIT], value_sum[UNIT:])
-            ):
-                unit = pair * NB + head * 4 + quarter
-                units[unit, 0:UNIT, :] = data.astype(BF16)
-                units[unit, UNIT:MSG, :] = stats
-        if step == 0:
-            pl.semaphore_wait(barrier, PLANE + NZ - 2)
-        for db in db_order:
-            if dx or db:
-                rs_copy(dx, db).start()
-
+    near[1, WIDTH:, :] = value_t
+    copies[0].wait()
+    dx_order = (2, 1, 3, 0)
+    heads = [(x + dx) & (NX - 1) for dx in dx_order]
+    maps = [ws[2 * p + c] for p in heads]
+    own = []
+    for p, slot_map in zip(heads, maps):
+        top, total, weight = block_weights(kv_t[0, p, c], slot_map)
+        paired = jnp.concatenate([kv_t[0, p, c], kv_t[1, p, c]], axis=0)
+        own.append((top, total, dot(paired, weight)))
+    swap_copy(0).wait_recv()
+    swap_copy(1).wait_recv()
+    others = [block_weights(other_t[0, p], slot_map) for p, slot_map in zip(heads, maps)]
+    for p, (own_top, own_total, own_sums), (top, total, weight) in zip(heads, own, others):
+        paired = jnp.concatenate([other_t[0, p], other_t[1, p]], axis=0)
+        joint = jnp.maximum(own_top, top)
+        own_scale, scale = jnp.exp(own_top - joint), jnp.exp(top - joint)
+        sums = own_scale * own_sums + scale * dot(paired, weight)
+        key_sum, value_sum = sums[:HEAD_DIM], sums[HEAD_DIM:]
+        key_sum = key_sum - jnp.mean(key_sum, axis=0, keepdims=True)
+        stats = stats_block(joint, own_scale * own_total + scale * total).astype(BF16)
+        for quarter, data in enumerate(
+            (key_sum[:UNIT], key_sum[UNIT:], value_sum[:UNIT], value_sum[UNIT:])
+        ):
+            units[p * NY + quarter, 0:UNIT, :] = data.astype(BF16)
+            units[p * NY + quarter, UNIT:MSG, :] = stats
+    turn = jnp.where(x == 3, 2, jnp.where(x == 2, 0, x))
+    places = [lax.rem(turn + k, 3) for k in (1, 2, 0)]
+    for tx in [place + (place >> 1) for place in places] + [2]:
+        dx = (tx + NX - x) & (NX - 1)
+        pl.when(dx != 0)(lambda dx=dx: pl.semaphore_wait(column.at[dx], 1))
+        for dy in (2, 1, 3):
+            rs_copy(dx, dy).start()
+        pl.when(dx != 0)(rs_copy(dx, 0).start)
+
+    pl.semaphore_wait(upward.at[0], 1)
+    pass_on(upward.at[1], 1)
+    pl.semaphore_wait(downward.at[0], 1)
+    pass_on(downward.at[1], NZ - 1)
     for head in range(HEADS):
         rows = slice(head * HEAD_DIM, (head + 1) * HEAD_DIM)
-        values = key_t[rows, :].astype(F32)
+        values = kv_t[0, head // 2, head % 2].astype(F32)
         center = values - jnp.mean(values, axis=0, keepdims=True)
         spread = jnp.mean(center * center, axis=0, keepdims=True)
         near[1, rows, :] = (center * lax.rsqrt(spread + 1e-05)).astype(BF16)
     pl.when(last)(lambda: relay_copy(0).start())
     pl.when(first)(lambda: relay_copy(1).start())
+    pl.semaphore_wait(upward.at[1], 1)
+    pass_on(upward.at[2], 1)
     copies[4].wait()
     query = dot(tok[...], wq[...]).astype(BF16).astype(F32) * (1.0 / HEAD_DIM**0.5)
     query_t[...] = query.astype(BF16).T
 
+    pl.semaphore_wait(downward.at[1], 1)
+    pl.semaphore_wait(upward.at[2], 1)
+
     running = None
     for dx in (0, 1, 3, 2):
         low = 1 if dx == 0 else 0
-        group_wait(rs_in.at[pl.ds(dx * NB + low, NB - low), pl.ds(0, MSG)], rs_recv.at[dx])
+        group_wait(rs_in.at[pl.ds(dx * NY + low, NY - low), pl.ds(0, MSG)], rs_recv.at[dx])
         parts = [
             (lambda k=k: rs_in[k, UNIT:MSG, :], lambda k=k: rs_in[k, 0:UNIT, :])
-            for k in range(dx * NB + low, (dx + 1) * NB)
+            for k in range(dx * NY + low, (dx + 1) * NY)
         ]
         if dx == 0:
-            parts.append((lambda: units[me, UNIT:MSG, :], lambda: units[me, 0:UNIT, :]))
+            mine = x * NY + y
+            parts.append((lambda: units[mine, UNIT:MSG, :], lambda: units[mine, 0:UNIT, :]))
         running = merge(parts, running)
     top, total, sums = running
     z_out[0:UNIT, :] = sums.astype(BF16)
@@ -285,7 +325,7 @@
     ]
     parts.append((lambda: z_out[UNIT:MSG, :], lambda: z_out[0:UNIT, :]))
     top, total, sums = merge(parts)
-    divisor = jnp.where((b & 3) >= 2, total, 1.0)
+    divisor = jnp.where(y >= 2, total, 1.0)
     slots[me] = (sums / divisor).astype(BF16)
     for dx in (2, 1, 3, 0):
         for db in db_order:
@@ -346,7 +386,9 @@
         columns = pl.ds(pl.multiple_of(pair * 2 * HEAD_DIM, 2 * HEAD_DIM), 2 * HEAD_DIM)
         out_ref[:, columns] = jnp.concatenate(results, axis=0).T
 
-    group_wait(rs_in.at[pl.ds(0, PLANE - 1), pl.ds(0, MSG)], rs_send.at[0])
+    group_wait(rs_in.at[pl.ds(0, CHIPS - 1), pl.ds(0, MSG)], rs_send.at[0])
+    swap_copy(0).wait_send()
+    swap_copy(1).wait_send()
     group_wait(z_in.at[pl.ds(0, NZ - 1), pl.ds(0, MSG)], z_send.at[0])
     group_wait(slots.at[pl.ds(0, PLANE - 1)], ag_send.at[0])
     halo_next.wait_send()
@@ -368,12 +410,11 @@
             pltpu.VMEM((D, WIDTH), BF16),
             pltpu.VMEM((HEADS, HEAD_DIM, SLOTS), BF16),
             dma((5,)),
-            pltpu.VMEM((HEADS // 2, 2 * HEAD_DIM, 2 * SLOTS), BF16),
-            pltpu.VMEM((ROWS, WIDTH), BF16),
+            pltpu.VMEM((2, NX, 2, HEAD_DIM, ROWS), BF16),
+            pltpu.VMEM((2, NX, HEAD_DIM, ROWS), BF16),
             pltpu.VMEM((WIDTH, ROWS), BF16),
-            pltpu.VMEM((WIDTH, ROWS), BF16),
-            pltpu.VMEM((PLANE, SLOT_ROWS, SLOTS), BF16),
-            pltpu.VMEM((PLANE, SLOT_ROWS, SLOTS), BF16),
+            pltpu.VMEM((CHIPS, SLOT_ROWS, SLOTS), BF16),
+            pltpu.VMEM((CHIPS, SLOT_ROWS, SLOTS), BF16),
             pltpu.VMEM((SLOT_ROWS, SLOTS), BF16),
             pltpu.VMEM((NZ, SLOT_ROWS, SLOTS), BF16),
             pltpu.VMEM((PLANE, UNIT, SLOTS), BF16),
@@ -382,6 +423,11 @@
             pltpu.VMEM((WIDTH, ROWS), F32),
             pltpu.VMEM((HEADS, 8, ROWS), F32),
             pltpu.VMEM((HEADS, 8, ROWS), F32),
+            pltpu.SemaphoreType.REGULAR((NX,)),
+            pltpu.SemaphoreType.REGULAR((3,)),
+            pltpu.SemaphoreType.REGULAR((2,)),
+            dma((2,)),
+            dma((2,)),
             dma((1,)),
             dma((NX,)),
             dma((1,)),

time: 30.6 us -> 29.6 us (0.967)
  Pallas kernels: 29.5 us -> 28.5 us
    pallas_call x1, Pallas kernels: 29.5 us -> 28.5 us  [per_device(): pl.pallas_call(layer, out_shape=jax.ShapeDtypeStruct((ROWS, WIDTH), BF16)...]
where the time goes in v4:
time: 29.6 us; the launch traced here: 29.5 us
  Pallas kernels  28.5 us (96%)
  matrix products  1.02 us (3%)
    pallas_call x1, Pallas kernels, per_device(): pl.pallas_call(layer, out_shape=jax.ShapeDtypeStruct((ROWS, WIDTH), BF16)...  28.5 us
    dot_general x1, matrix products, per_device(): return jnp.dot(attended, w_out, preferred_element_type=F32).astype(BF16)  1.02 us

profile of v4, /device:TPU:1, one launch (start us, length us, event | category | flops | bytes accessed | tf_op | source)
XLA Modules:
  0.0 29.5 jit_solution(13558073850709367523)
XLA Ops:
  0.0 0.0 copy-start
  0.0 28.5 %layer.1 = bf16[128,512]{1,0:T(8,128)(2,1)S(1)} custom-call(bf16[128,1024]{1,0:T(8,128)(2,1)} %tok_hbm.1, bf16[1024,512]{1,0:T(8,128)(2,1)} %wq_hbm.1, bf16[1024,512]{1,0:T(8,128)(2,1)} %wk_hbm.1, bf16[1024,512]{1,0:T(8,128)(2,1)} %wv_hbm.1, bf16[8,64,128]{2,1,0:T(8,128)(2,1)} %ws_hbm.1), custom_call_target="tpu_custom_call" | custom-call | tf_op jit(solution)/shard_map/layer/pallas_call | solution.py:401
  28.5 0.0 copy-done
  28.5 1.0 %convolution_convert_fusion = bf16[128,1024]{1,0:T(8,128)(2,1)} fusion(bf16[128,512]{1,0:T(8,128)(2,1)S(1)} %layer.1, bf16[512,1024]{1,0:T(8,128)(2,1)S(1)} %copy-done), kind=kOutput, calls=%fused_computation | convolution fusion | flops 134348800 | bytes 1441792 | tf_op jit(solution)/shard_map/dot_general | solution.py:447
Async XLA Ops:
  0.0 28.5 %copy-start = (bf16[512,1024]{1,0:T(8,128)(2,1)S(1)}, bf16[512,1024]{1,0:T(8,128)(2,1)}, u32[]{:S(2)}) copy-start(bf16[512,1024]{1,0:T(8,128)(2,1)} %param.11) | copy-start | bytes 3145732

commit v5 on v4

--- a/solution.py
+++ b/solution.py
@@ -149,7 +149,7 @@
 
     def swap_copy(i):
         return pltpu.make_async_remote_copy(
-            src_ref=kv_t.at[i, :, 1 - c],
+            src_ref=kv_t.at[i, 1 - c],
             dst_ref=other_t.at[i],
             send_sem=swap_send.at[i],
             recv_sem=swap_recv.at[i],
@@ -225,10 +225,12 @@
 
     copies[1].wait()
     copies[2].wait()
-    kv_t[0] = dot(tok[...], wk[...]).astype(BF16).T.reshape(NX, 2, HEAD_DIM, ROWS)
+    by_head = dot(tok[...], wk[...]).astype(BF16).T.reshape(NX, 2, HEAD_DIM, ROWS)
+    kv_t[0, 0], kv_t[0, 1] = by_head[:, 0], by_head[:, 1]
     copies[3].wait()
     value_t = dot(tok[...], wv[...]).astype(BF16).T
-    kv_t[1] = value_t.reshape(NX, 2, HEAD_DIM, ROWS)
+    by_head = value_t.reshape(NX, 2, HEAD_DIM, ROWS)
+    kv_t[1, 0], kv_t[1, 1] = by_head[:, 0], by_head[:, 1]
     wait_greetings()
     swap_copy(0).start()
     swap_copy(1).start()
@@ -240,8 +242,8 @@
     maps = [ws[2 * p + c] for p in heads]
     own = []
     for p, slot_map in zip(heads, maps):
-        top, total, weight = block_weights(kv_t[0, p, c], slot_map)
-        paired = jnp.concatenate([kv_t[0, p, c], kv_t[1, p, c]], axis=0)
+        top, total, weight = block_weights(kv_t[0, c, p], slot_map)
+        paired = jnp.concatenate([kv_t[0, c, p], kv_t[1, c, p]], axis=0)
         own.append((top, total, dot(paired, weight)))
     swap_copy(0).wait_recv()
     swap_copy(1).wait_recv()
@@ -274,7 +276,7 @@
     pass_on(downward.at[1], NZ - 1)
     for head in range(HEADS):
         rows = slice(head * HEAD_DIM, (head + 1) * HEAD_DIM)
-        values = kv_t[0, head // 2, head % 2].astype(F32)
+        values = kv_t[0, head % 2, head // 2].astype(F32)
         center = values - jnp.mean(values, axis=0, keepdims=True)
         spread = jnp.mean(center * center, axis=0, keepdims=True)
         near[1, rows, :] = (center * lax.rsqrt(spread + 1e-05)).astype(BF16)
@@ -410,7 +412,7 @@
             pltpu.VMEM((D, WIDTH), BF16),
             pltpu.VMEM((HEADS, HEAD_DIM, SLOTS), BF16),
             dma((5,)),
-            pltpu.VMEM((2, NX, 2, HEAD_DIM, ROWS), BF16),
+            pltpu.VMEM((2, 2, NX, HEAD_DIM, ROWS), BF16),
             pltpu.VMEM((2, NX, HEAD_DIM, ROWS), BF16),
             pltpu.VMEM((WIDTH, ROWS), BF16),
             pltpu.VMEM((CHIPS, SLOT_ROWS, SLOTS), BF16),

time: 29.6 us -> 29.6 us (level)
  no operation moved by 1% of the time
where the time goes in v5:
time: 29.6 us; the launch traced here: 29.5 us
  Pallas kernels  28.4 us (96%)
  matrix products  1.02 us (3%)
    pallas_call x1, Pallas kernels, per_device(): pl.pallas_call(layer, out_shape=jax.ShapeDtypeStruct((ROWS, WIDTH), BF16)...  28.4 us
    dot_general x1, matrix products, per_device(): return jnp.dot(attended, w_out, preferred_element_type=F32).astype(BF16)  1.02 us

profile of v5, /device:TPU:1, one launch (start us, length us, event | category | flops | bytes accessed | tf_op | source)
XLA Modules:
  0.0 29.5 jit_solution(9405892564082857227)
XLA Ops:
  0.0 0.0 copy-start
  0.0 28.4 %layer.1 = bf16[128,512]{1,0:T(8,128)(2,1)S(1)} custom-call(bf16[128,1024]{1,0:T(8,128)(2,1)} %tok_hbm.1, bf16[1024,512]{1,0:T(8,128)(2,1)} %wq_hbm.1, bf16[1024,512]{1,0:T(8,128)(2,1)} %wk_hbm.1, bf16[1024,512]{1,0:T(8,128)(2,1)} %wv_hbm.1, bf16[8,64,128]{2,1,0:T(8,128)(2,1)} %ws_hbm.1), custom_call_target="tpu_custom_call" | custom-call | tf_op jit(solution)/shard_map/layer/pallas_call | solution.py:403
  28.5 0.0 copy-done
  28.5 1.0 %convolution_convert_fusion = bf16[128,1024]{1,0:T(8,128)(2,1)} fusion(bf16[128,512]{1,0:T(8,128)(2,1)S(1)} %layer.1, bf16[512,1024]{1,0:T(8,128)(2,1)S(1)} %copy-done), kind=kOutput, calls=%fused_computation | convolution fusion | flops 134348800 | bytes 1441792 | tf_op jit(solution)/shard_map/dot_general | solution.py:449
Async XLA Ops:
  0.0 28.5 %copy-start = (bf16[512,1024]{1,0:T(8,128)(2,1)S(1)}, bf16[512,1024]{1,0:T(8,128)(2,1)}, u32[]{:S(2)}) copy-start(bf16[512,1024]{1,0:T(8,128)(2,1)} %param.11) | copy-start | bytes 3145732

commit v6 on v5

--- a/solution.py
+++ b/solution.py
@@ -227,12 +227,12 @@
     copies[2].wait()
     by_head = dot(tok[...], wk[...]).astype(BF16).T.reshape(NX, 2, HEAD_DIM, ROWS)
     kv_t[0, 0], kv_t[0, 1] = by_head[:, 0], by_head[:, 1]
+    wait_greetings()
+    swap_copy(0).start()
     copies[3].wait()
     value_t = dot(tok[...], wv[...]).astype(BF16).T
     by_head = value_t.reshape(NX, 2, HEAD_DIM, ROWS)
     kv_t[1, 0], kv_t[1, 1] = by_head[:, 0], by_head[:, 1]
-    wait_greetings()
-    swap_copy(0).start()
     swap_copy(1).start()
     copies[4].start()
     near[1, WIDTH:, :] = value_t
@@ -246,8 +246,8 @@
         paired = jnp.concatenate([kv_t[0, c, p], kv_t[1, c, p]], axis=0)
         own.append((top, total, dot(paired, weight)))
     swap_copy(0).wait_recv()
+    others = [block_weights(other_t[0, p], slot_map) for p, slot_map in zip(heads, maps)]
     swap_copy(1).wait_recv()
-    others = [block_weights(other_t[0, p], slot_map) for p, slot_map in zip(heads, maps)]
     for p, (own_top, own_total, own_sums), (top, total, weight) in zip(heads, own, others):
         paired = jnp.concatenate([other_t[0, p], other_t[1, p]], axis=0)
         joint = jnp.maximum(own_top, top)

time: 29.6 us -> 29.6 us (level)
  no operation moved by 1% of the time
where the time goes in v6:
time: 29.6 us; the launch traced here: 29.5 us
  Pallas kernels  28.4 us (96%)
  matrix products  1.02 us (3%)
    pallas_call x1, Pallas kernels, per_device(): pl.pallas_call(layer, out_shape=jax.ShapeDtypeStruct((ROWS, WIDTH), BF16)...  28.4 us
    dot_general x1, matrix products, per_device(): return jnp.dot(attended, w_out, preferred_element_type=F32).astype(BF16)  1.02 us

profile of v6, /device:TPU:1, one launch (start us, length us, event | category | flops | bytes accessed | tf_op | source)
XLA Modules:
  0.0 29.5 jit_solution(12232783463605324401)
XLA Ops:
  0.0 0.0 copy-start
  0.0 28.4 %layer.1 = bf16[128,512]{1,0:T(8,128)(2,1)S(1)} custom-call(bf16[128,1024]{1,0:T(8,128)(2,1)} %tok_hbm.1, bf16[1024,512]{1,0:T(8,128)(2,1)} %wq_hbm.1, bf16[1024,512]{1,0:T(8,128)(2,1)} %wk_hbm.1, bf16[1024,512]{1,0:T(8,128)(2,1)} %wv_hbm.1, bf16[8,64,128]{2,1,0:T(8,128)(2,1)} %ws_hbm.1), custom_call_target="tpu_custom_call" | custom-call | tf_op jit(solution)/shard_map/layer/pallas_call | solution.py:403
  28.4 0.0 copy-done
  28.4 1.0 %convolution_convert_fusion = bf16[128,1024]{1,0:T(8,128)(2,1)} fusion(bf16[128,512]{1,0:T(8,128)(2,1)S(1)} %layer.1, bf16[512,1024]{1,0:T(8,128)(2,1)S(1)} %copy-done), kind=kOutput, calls=%fused_computation | convolution fusion | flops 134348800 | bytes 1441792 | tf_op jit(solution)/shard_map/dot_general | solution.py:449
Async XLA Ops:
  0.0 28.4 %copy-start = (bf16[512,1024]{1,0:T(8,128)(2,1)S(1)}, bf16[512,1024]{1,0:T(8,128)(2,1)}, u32[]{:S(2)}) copy-start(bf16[512,1024]{1,0:T(8,128)(2,1)} %param.11) | copy-start | bytes 3145732
